TPU v7x, 1024 devices: a whole 8x8x8 slice. The times are simulated.
1024 devices in a mesh: loop: 64 (over z_lo, x, core), tensor: 16 (over y, z_hi).
Axes of the slice: x: 8, y: 8, z: 8 (z_hi: 2, z_lo: 4; z = z_hi * 4 + z_lo), core: 2. Of those that a mesh axis runs over, the one named last changes fastest.
Arguments:
- grad_out: bfloat16 [8192, 4096], P('loop', 'tensor'), may hold values from -6 to 6
- saved_hidden: bfloat16 [1664, 32768], P('tensor', 'loop'), may hold values from -6 to 6
- picked_tokens: int32 [2, 1664], replicated, may hold values from 0 to 8191, as said below
- gate_values: float32 [2, 1664], replicated, may hold values from 0.25 to 1
- in_weight: bfloat16 [4096, 32768], P(None, 'loop'), may hold values from -0.09375 to 0.09375
- out_weight: bfloat16 [32768, 4096], P('loop'), may hold values from -0.046875 to 0.046875
Outputs:
- input_grad: bfloat16 [8192, 4096], P('loop', 'tensor')
Inputs may be any that keep to these rules, and one draw needn't show every extreme that they name: Each row picked_tokens[e] lists 1664 distinct token indices in ascending order; among the 128 tokens of one loop index (an aligned block) it names at most 28, and in every row some block holds exactly 28.
All inputs are finite; a program needn't handle non-finite values.
Results may differ from a plain program's by a relative error of at most 0.0032.
Values may be sent and summed in bfloat16 or wider, within the bound.
A program may use at most 32 MiB of HBM per device.

v0:
```python
import math

import jax
import jax.numpy as jnp
from jax import lax
from jax.sharding import Mesh
from jax.sharding import PartitionSpec as P

MOST = 28
LOOP = ("loop_0", "loop_1", "loop_2")


slope_scale = math.sqrt(2.0 / math.pi)


def in_blocks(value, dim, peers):
    before, after = (value.shape[:dim], value.shape[dim + 1 :])
    return jnp.moveaxis(value.reshape(*before, peers, -1, *after), dim, 0)


def laid_out(pieces, dim):
    pieces = jnp.moveaxis(pieces, 0, dim)
    dims = pieces.shape
    return pieces.reshape(*dims[:dim], dims[dim] * dims[dim + 1], *dims[dim + 2 :])


def exchange_in_order(pieces, axes, turns):
    inside = pieces.shape[1:]
    filled = pieces.reshape(*(lax.axis_size(a) for a in axes), *inside)
    for k in turns:
        filled = lax.all_to_all(filled, axes[k], k, k, tiled=True)
    return filled.reshape(-1, *inside)


def exchange_by_chip(value, groups, turns, split_dim, concat_dim):
    peers = lax.axis_size(groups[0]) * lax.axis_size(groups[1])
    pieces = in_blocks(value, split_dim, peers)
    return laid_out(exchange_in_order(pieces, groups, turns), concat_dim)


def gelu_slope(values):
    inner = slope_scale * (values + 0.044715 * values * values * values)
    bent = jnp.tanh(inner)
    return 0.5 * (1.0 + bent) + 0.5 * values * (1.0 - bent * bent) * slope_scale * (
        1.0 + 0.134145 * values * values
    )


def block_slots(ordered, offset, length, slot_count):
    list_length = ordered.shape[-1]
    first_slot = jnp.sum((ordered < offset).astype(jnp.int32), axis=-1, keepdims=True)
    positions = first_slot + jnp.arange(slot_count, dtype=jnp.int32)
    clamped = jnp.minimum(positions, list_length - 1)
    local_rows = jnp.take_along_axis(ordered, clamped, axis=-1) - offset
    inside = (positions < list_length) & (local_rows < length)
    return (clamped, local_rows, inside)


def shards(grad_out, saved_hidden, picked_tokens, gate_values, in_weight, out_weight):
    home_rows, feature_cols = grad_out.shape
    loop_size = lax.axis_size(LOOP)
    expert_count = picked_tokens.shape[0]
    capacity = picked_tokens.shape[1]
    group_size = loop_size // expert_count
    loop_index = lax.axis_index(LOOP)
    expert_id = loop_index // group_size
    home_start = loop_index * home_rows
    own_picks = lax.dynamic_index_in_dim(picked_tokens, expert_id, 0, keepdims=False)
    block_starts = jnp.arange(loop_size, dtype=jnp.int32) * home_rows
    first_mine = jnp.sum((own_picks[None, :] < block_starts[:, None]).astype(jnp.int32), axis=1)
    clamped, local_rows, inside = block_slots(picked_tokens, home_start, home_rows, MOST)
    fetched = jnp.take(grad_out, jnp.clip(local_rows, 0, home_rows - 1), axis=0)
    slot_gates = jnp.take_along_axis(gate_values, clamped, axis=1)
    outgoing = jnp.where(
        inside[:, :, None], slot_gates[:, :, None] * fetched.astype(jnp.float32), 0.0
    ).astype(jnp.bfloat16)
    outgoing = jnp.repeat(outgoing, group_size, axis=0)
    arrived = exchange_by_chip(outgoing, (("loop_0", "loop_1"), "loop_2"), (1, 0), 0, 0)
    source_block = own_picks // home_rows
    matches = source_block[:, None] == jnp.arange(loop_size, dtype=jnp.int32)[None, :]
    block_first = jnp.sum(jnp.where(matches, first_mine[None, :], 0), axis=1)
    slot_index = source_block * MOST + jnp.arange(capacity, dtype=jnp.int32) - block_first
    scaled = jnp.take(arrived.reshape(loop_size * MOST, feature_cols), slot_index, axis=0)
    wide_rows = lax.all_to_all(scaled, "tensor", split_axis=0, concat_axis=1, tiled=True)
    act_grad = lax.dot_general(
        wide_rows, out_weight, (((1,), (1,)), ((), ())), preferred_element_type=jnp.float32
    )
    pre_grad = (act_grad * gelu_slope(saved_hidden.astype(jnp.float32))).astype(jnp.bfloat16)
    partial_grad = lax.dot_general(
        pre_grad, in_weight, (((1,), (1,)), ((), ())), preferred_element_type=jnp.float32
    )
    returned = lax.all_to_all(partial_grad, "tensor", split_axis=1, concat_axis=0, tiled=True)
    last_mine = jnp.sum(
        (own_picks[None, :] < block_starts[:, None] + home_rows).astype(jnp.int32), axis=1
    )
    positions = first_mine[:, None] + jnp.arange(MOST, dtype=jnp.int32)[None, :]
    inside_out = positions < last_mine[:, None]
    fetched_back = jnp.take(returned, jnp.minimum(positions, capacity - 1), axis=0)
    sending = jnp.where(inside_out[:, :, None], fetched_back, 0.0)
    landed = lax.all_to_all(sending, LOOP, split_axis=0, concat_axis=0, tiled=True)
    home_clamped, home_local, home_inside = block_slots(picked_tokens, home_start, home_rows, MOST)
    target = jnp.repeat(jnp.where(home_inside, home_local, home_rows), group_size, axis=0)
    summed = (
        jnp.zeros((home_rows, feature_cols), jnp.float32)
        .at[target.reshape(-1)]
        .add(landed.reshape(-1, feature_cols), mode="drop")
    )
    return (grad_out.astype(jnp.float32) + summed).astype(jnp.bfloat16)


def solution(mesh):
    torus = Mesh(
        mesh.devices.reshape(4, 8, 2, mesh.shape["tensor"]),
        ("loop_0", "loop_1", "loop_2", "tensor"),
    )
    placed = (P(LOOP, "tensor"), P("tensor", LOOP), P(), P(), P(None, LOOP), P(LOOP, None))
    return jax.shard_map(
        shards, mesh=torus, in_specs=placed, out_specs=P(LOOP, "tensor"), check_vma=False
    )
```

profile of v0, /device:TPU:96, one launch (start us, length us, event | category | flops | bytes accessed | tf_op | source)
XLA Modules:
  0.0 265.8 jit_solution(10965642970262400763)
XLA Ops:
  0.0 0.0 copy-start
  0.0 0.8 fusion.25
  0.9 0.1 fusion.37
  0.9 0.1 reshape.406
  1.0 1.8 gather_fusion.4
  2.8 0.1 reshape.409
  2.9 0.1 compare_select_fusion.9
  3.0 0.7 broadcast_select_fusion.3
  3.7 0.1 copy.23
  3.8 0.1 copy.25
  3.9 0.1 reshape.361
  4.0 1.5 gather_fusion
  5.5 0.1 reshape.383
  5.6 0.0 copy-done
  5.6 1.1 gather_fusion.3
  6.7 0.1 reshape.386
  6.7 0.1 broadcast_select_fusion.2
  6.8 0.1 copy.24
  6.9 0.2 select_convert_fusion
  7.1 0.1 broadcast_in_dim.120
  7.3 4.5 %all_to_all.50 = bf16[32,2,1,28,256]{4,0,3,2,1:T(8,128)(2,1)S(1)} all-to-all(bf16[32,2,1,28,256]{4,0,3,2,1:T(8,128)(2,1)S(1)} %broadcast_in_dim.120), channel_id=1, replica_groups=mesh['loop_0'=4,'loop_1'=8,'loop_2'=2,'tensor'=16] {'loop_2'}, dimensions={1} | all-to-all | bytes 1835008 | tf_op jit(solution)/shard_map/all_to_all | solution.py:31
  11.7 0.0 copy-start.1
  11.7 1.9 copy.27
  13.6 15.3 %all-to-all-start.1 = ((bf16[32,2,1,28,256]{4,1,3,2,0:T(2,128)(2,1)}), bf16[32,2,1,28,256]{4,1,3,2,0:T(2,128)(2,1)S(1)}, u32[]{:S(2)}, u32[]{:S(2)}) async-start(bf16[32,2,1,28,256]{4,1,3,2,0:T(2,128)(2,1)} %copy.27), calls=%async_computation.1 | async-start | bytes 1835008 | tf_op jit(solution)/shard_map/all_to_all | solution.py:31
  28.9 0.0 copy-done.1
  29.0 0.1 lt.165
  29.1 0.2 convert_reduce_fusion
  29.3 0.1 select_reduce_fusion
  29.5 0.1 reduce_sum.48
  29.6 0.1 fusion.34
  29.7 26.0 %all-to-all-done.1 = bf16[32,2,1,28,256]{4,1,3,2,0:T(2,128)(2,1)S(1)} async-done(((bf16[32,2,1,28,256]{4,1,3,2,0:T(2,128)(2,1)}), bf16[32,2,1,28,256]{4,1,3,2,0:T(2,128)(2,1)S(1)}, u32[]{:S(2)}, u32[]{:S(2)}) %all-to-all-start.1) | async-done | bytes 917536 | tf_op jit(solution)/shard_map/all_to_all | solution.py:31
  55.7 0.2 copy.28
  55.9 0.2 reshape_reshape_reshape.4
  56.1 5.6 %gather_fusion.1 = bf16[1664,256]{1,0:T(8,128)(2,1)S(1)} fusion(bf16[1792,256]{1,0:T(8,128)(2,1)S(1)} %reshape_reshape_reshape.4, s32[2048]{0:T(1024)S(1)} %pad_clamp_fusion.1), kind=kCustom, calls=%fused_computation.2 | custom fusion | bytes 1710592 | tf_op jit(solution)/shard_map/jit(_take)/gather | solution.py:83
  61.7 0.3 broadcast_select_fusion
  62.0 0.0 copy-start.3
  62.0 38.3 %all_to_all.51 = bf16[16,104,256]{2,1,0:T(8,128)(2,1)S(1)} all-to-all(bf16[16,104,256]{2,1,0:T(8,128)(2,1)S(1)} %broadcast_select_fusion), channel_id=1, replica_groups=mesh['loop_0'=4,'loop_1'=8,'loop_2'=2,'tensor'=16] {'tensor'}, dimensions={0} | all-to-all | bytes 1703936 | tf_op jit(solution)/shard_map/all_to_all | solution.py:84
  100.3 0.1 copy.32
  100.4 0.0 copy-done.3
  100.4 6.2 %fusion.1 = f32[104,4096]{1,0:T(8,128)S(1)} fusion(bf16[4096,512]{1,0:T(8,128)(2,1)} %param.12, bf16[104,4096]{1,0:T(8,128)(2,1)S(1)} %bitcast.38, bf16[512,4096]{1,0:T(8,128)(2,1)} %param.13, bf16[104,512]{1,0:T(8,128)(2,1)S(1)} %copy-done.3), kind=kOutput, calls=%fused_computation.10 | convolution fusion | flops 873480192 | bytes 11051008 | tf_op jit(solution)/shard_map/dot_general | solution.py:89
  106.6 1.3 copy.35
  107.9 7.4 %all-to-all-start.3 = ((f32[104,16,256]{2,0,1:T(8,128)}), f32[104,16,256]{2,0,1:T(8,128)S(1)}, u32[]{:S(2)}, u32[]{:S(2)}) async-start(f32[104,16,256]{2,0,1:T(8,128)} %bitcast.34), calls=%async_computation.3 | async-start | bytes 3407872 | tf_op jit(solution)/shard_map/all_to_all | solution.py:92
  115.4 0.1 compare_select_fusion
  115.4 0.1 reshape.377
  115.5 0.6 pad_clamp_fusion
  116.2 0.7 fusion.21
  116.8 50.8 %all-to-all-done.3 = f32[104,16,256]{2,0,1:T(8,128)S(1)} async-done(((f32[104,16,256]{2,0,1:T(8,128)}), f32[104,16,256]{2,0,1:T(8,128)S(1)}, u32[]{:S(2)}, u32[]{:S(2)}) %all-to-all-start.3) | async-done | bytes 1703968 | tf_op jit(solution)/shard_map/all_to_all | solution.py:92
  167.7 4.7 %gather_fusion.2 = f32[1792,256]{1,0:T(8,128)S(1)} fusion(f32[1664,256]{1,0:T(8,128)S(1)} %bitcast.35, s32[2048]{0:T(1024)} %pad_clamp_fusion), kind=kCustom, calls=%fused_computation.3 | custom fusion | bytes 3677184 | tf_op jit(solution)/shard_map/jit(_take)/gather | solution.py:98
  172.4 0.0 copy-start.4
  172.4 0.0 copy-start.5
  172.4 1.5 reshape.376
  174.0 0.0 copy-done.4
  174.0 0.0 copy-done.5
  174.0 3.0 %select_select_fusion = f32[64,28,256]{2,1,0:T(8,128)} fusion(f32[64,28,256]{2,1,0:T(8,128)} %reshape.376, pred[64,28]{1,0:T(8,128)(4,1)S(1)} %copy-done.5, pred[64,28]{1,0:T(8,128)(4,1)S(1)} %copy-done.4), kind=kLoop, calls=%fused_computation.6 | loop fusion | flops 917504 | bytes 3673600 | tf_op jit(solution)/shard_map/jit(_where)/select_n | solution.py:99
  176.9 0.0 copy-start.2
  176.9 0.0 copy-start.6
  176.9 22.9 %all-to-all-start.4 = ((f32[64,28,256]{2,1,0:T(8,128)}), f32[64,28,256]{2,1,0:T(8,128)S(1)}, u32[]{:S(2)}, u32[]{:S(2)}) async-start(f32[64,28,256]{2,1,0:T(8,128)} %select_select_fusion), calls=%async_computation.4 | async-start | bytes 4194304 | tf_op jit(solution)/shard_map/all_to_all | solution.py:100
  199.8 0.0 copy-done.2
  199.8 0.0 copy-done.6
  199.9 0.1 reshape_reshape.3
  200.0 51.5 %all-to-all-done.4 = f32[64,28,256]{2,1,0:T(8,128)S(1)} async-done(((f32[64,28,256]{2,1,0:T(8,128)}), f32[64,28,256]{2,1,0:T(8,128)S(1)}, u32[]{:S(2)}, u32[]{:S(2)}) %all-to-all-start.4) | async-done | bytes 1835040 | tf_op jit(solution)/shard_map/all_to_all | solution.py:100
  251.5 1.4 reshape.393
  252.9 12.2 %scatter_fusion = f32[128,256]{1,0:T(8,128)S(1)} fusion(f32[128,256]{1,0:T(8,128)S(1)} %convert_element_type.28, s32[1792]{0:T(1024)S(1)} %fusion.33, f32[1792,256]{1,0:T(8,128)} %reshape.393), kind=kCustom, calls=%fused_computation.5 | custom fusion | flops 458752 | bytes 5512192 | tf_op jit(solution)/shard_map/scatter-add | solution.py:106
  265.1 0.6 convert_element_type.36
  (12 shorter events, 0.2 us)
Async XLA Ops:
  0.0 5.6 %copy-start = (f32[2,1664]{1,0:T(2,128)S(1)}, f32[2,1664]{1,0:T(2,128)}, u32[]{:S(2)}) copy-start(f32[2,1664]{1,0:T(2,128)} %param.11) | copy-start | bytes 39940
  11.7 17.2 %copy-start.1 = (s32[2,1664]{1,0:T(2,128)S(1)}, s32[2,1664]{1,0:T(2,128)}, u32[]{:S(2)}) copy-start(s32[2,1664]{1,0:T(2,128)} %param.10) | copy-start | bytes 39940
  13.6 42.1 %all-to-all-start.1 = ((bf16[32,2,1,28,256]{4,1,3,2,0:T(2,128)(2,1)}), bf16[32,2,1,28,256]{4,1,3,2,0:T(2,128)(2,1)S(1)}, u32[]{:S(2)}, u32[]{:S(2)}) async-start(bf16[32,2,1,28,256]{4,1,3,2,0:T(2,128)(2,1)} %copy.27), calls=%async_computation.1 | async-start | bytes 1835008 | tf_op jit(solution)/shard_map/all_to_all | solution.py:31
  62.0 38.4 %copy-start.3 = (bf16[104,512]{1,0:T(8,128)(2,1)S(1)}, bf16[104,512]{1,0:T(8,128)(2,1)}, u32[]{:S(2)}) copy-start(bf16[104,512]{1,0:T(8,128)(2,1)} %param.9) | copy-start | bytes 319492
  107.9 59.7 %all-to-all-start.3 = ((f32[104,16,256]{2,0,1:T(8,128)}), f32[104,16,256]{2,0,1:T(8,128)S(1)}, u32[]{:S(2)}, u32[]{:S(2)}) async-start(f32[104,16,256]{2,0,1:T(8,128)} %bitcast.34), calls=%async_computation.3 | async-start | bytes 3407872 | tf_op jit(solution)/shard_map/all_to_all | solution.py:92
  172.4 1.6 copy-start.4
  172.4 1.6 copy-start.5
  176.9 22.9 %copy-start.2 = (bf16[128,256]{1,0:T(8,128)(2,1)S(1)}, bf16[128,256]{1,0:T(8,128)(2,1)}, u32[]{:S(2)}) copy-start(bf16[128,256]{1,0:T(8,128)(2,1)} %param.8) | copy-start | bytes 196612
  176.9 22.9 %copy-start.6 = (s32[2,28]{1,0:T(2,128)S(1)}, s32[2,28]{1,0:T(2,128)}, u32[]{:S(2)}) copy-start(s32[2,28]{1,0:T(2,128)} %get-tuple-element.10) | copy-start | bytes 676
  176.9 74.5 %all-to-all-start.4 = ((f32[64,28,256]{2,1,0:T(8,128)}), f32[64,28,256]{2,1,0:T(8,128)S(1)}, u32[]{:S(2)}, u32[]{:S(2)}) async-start(f32[64,28,256]{2,1,0:T(8,128)} %select_select_fusion), calls=%async_computation.4 | async-start | bytes 4194304 | tf_op jit(solution)/shard_map/all_to_all | solution.py:100
where the time goes:
time: 267 us; the launch traced here: 266 us
  waiting for transfers between devices  128 us (48%)
  starting transfers between devices  45.6 us (17%)
  blocking collectives  42.8 us (16%)
  local copies, waits for them, and re-layouts  22.6 us (8%)
  other arithmetic  20 us (7%)
  matrix products  6.18 us (2%)
    all_to_all x1, waiting for transfers between devices, shards(): lax.all_to_all(sending, LOOP, split_axis=0, concat_axis=0, tiled=True)  51.5 us
    all_to_all x1, waiting for transfers between devices, shards(): lax.all_to_all(partial_grad, 'tensor', split_axis=1, concat_axis=0, tiled...  50.8 us
    all_to_all x1, blocking collectives, shards(): lax.all_to_all(scaled, 'tensor', split_axis=0, concat_axis=1, tiled=True)  38.3 us
    all_to_all x1, waiting for transfers between devices, exchange_in_order(): filled = lax.all_to_all(filled, axes[k], k, k, tiled=True)  26 us
    all_to_all x1, starting transfers between devices, shards(): lax.all_to_all(sending, LOOP, split_axis=0, concat_axis=0, tiled=True)  22.9 us
    all_to_all x1, starting transfers between devices, exchange_in_order(): filled = lax.all_to_all(filled, axes[k], k, k, tiled=True)  15.3 us
    scatter-add x1, other arithmetic, shards(): summed = jnp.zeros((home_rows, feature_cols), jnp.float32).at[target.resh...  12.2 us
    all_to_all x1, starting transfers between devices, shards(): lax.all_to_all(partial_grad, 'tensor', split_axis=1, concat_axis=0, tiled...  7.43 us
  transfers between devices with their start and end apart: 3, of which 3 were waited for; matrix products, arithmetic and copies ran while one was open for 1% of the time, Pallas kernels for 0%

commit v1 on v0

v1 whole, which is shorter than its diff:
```python
import functools
import math

import jax
import jax.numpy as jnp
from jax import lax
from jax.experimental import pallas as pl
from jax.experimental.pallas import tpu as pltpu
from jax.sharding import PartitionSpec as P

MOST = 28
SLOTS = 32
CORES = 2
PLANES = 2
CHUNKS = 3
MESH = pl.DeviceIdType.MESH

slope_scale = math.sqrt(2.0 / math.pi)


def gelu_slope(values):
    inner = slope_scale * (values + 0.044715 * values * values * values)
    bent = jnp.tanh(inner)
    return 0.5 * (1.0 + bent) + 0.5 * values * (1.0 - bent * bent) * slope_scale * (
        1.0 + 0.134145 * values * values
    )


def window_size(blocks, capacity, chunks):
    rows = capacity // chunks
    spare = MOST * blocks - capacity
    widest = 0
    for chunk in range(chunks):
        low = rows * chunk // MOST
        high = max(b for b in range(blocks) if max(0, MOST * b - spare) < rows * (chunk + 1))
        widest = max(widest, high - low + 1)
    return widest


def by_distance(ring):
    order = []
    for d in range(1, ring // 2 + 1):
        order.append(d)
        if ring - d != d:
            order.append(ring - d)
    return order


def dot_nt(a, b):
    return lax.dot_general(a, b, (((1,), (1,)), ((), ())), preferred_element_type=jnp.float32)


def dot_tn(a, b):
    return lax.dot_general(a, b, (((0,), (0,)), ((), ())), preferred_element_type=jnp.float32)


def dot_nn(a, b):
    return lax.dot_general(a, b, (((1,), (0,)), ((), ())), preferred_element_type=jnp.float32)


def split_exact(values):
    high = values.astype(jnp.bfloat16)
    low = (values - high.astype(jnp.float32)).astype(jnp.bfloat16)
    return high, low


def kernel(
    sizes,
    grad_ref,
    hidden_ref,
    picks_ref,
    gates_ref,
    chunk_ref,
    in_hbm,
    out_hbm,
    result_ref,
    in_ref,
    out_ref,
    slot_ref,
    arrive_ref,
    wide_ref,
    core_send,
    core_recv,
    plane_send,
    plane_recv,
    own_ref,
    ring_send,
    ring_recv,
    back_ref,
    home_ref,
    weight_sem,
    a_send,
    a_recv,
    bx_send,
    bx_recv,
    bz_send,
    bz_recv,
    bc_send,
    bc_recv,
    cc_send,
    cc_recv,
    cz_send,
    cz_recv,
    cx_send,
    cx_recv,
    d_send,
    d_recv,
):
    experts, chunks, blocks, ring, window = sizes
    block_rows, home_cols = grad_ref.shape
    rows, width = hidden_ref.shape
    features = in_ref.shape[0]
    capacity = picks_ref.shape[1]
    group = blocks // experts
    piece = features // group
    halves = group // chunks
    quarter = features // (CORES * PLANES)
    f32, bf16, i32 = jnp.float32, jnp.bfloat16, jnp.int32

    loop, chunk = lax.axis_index("loop"), lax.axis_index("tensor")
    expert = loop // group
    place = lax.rem(loop, group)
    plane = place // (ring * CORES)
    spot = lax.rem(place // CORES, ring)
    core = lax.rem(place, CORES)
    slice_id = core * (PLANES * ring) + plane * ring + spot
    slice_home = slice_id // halves
    slice_half = lax.rem(slice_id, halves)

    def start_of(t):
        return jnp.minimum(rows * t // MOST, blocks - window)

    def first_of(b):
        return (MOST * jnp.maximum(b - window + 1, 0) + rows - 1) // rows

    def loop_of(e, p, s, c):
        return e * group + (p * ring + s) * CORES + c

    def loop_of_slice(e, j):
        return loop_of(e, lax.rem(j // ring, PLANES), lax.rem(j, ring), j // (PLANES * ring))

    first = first_of(loop)
    begin = start_of(chunk)

    def at_slice(c, p, s):
        return pl.ds(pl.multiple_of((c * (PLANES * ring) + p * ring + s) * piece, piece), piece)

    def targets(body):
        for k in range(CHUNKS):
            t = first + k

            @pl.when((t < chunks) & (start_of(t) <= loop))
            def _():
                for e in range(experts):
                    for h in range(halves):
                        body(e, k, h, loop_of_slice(e, chunk * halves + h), t)

    weights = (
        pltpu.make_async_copy(out_hbm, out_ref, weight_sem.at[0]),
        pltpu.make_async_copy(in_hbm, in_ref, weight_sem.at[1]),
    )
    for copy in weights:
        copy.start()
    home_ref[...] = jnp.zeros_like(home_ref)

    barrier = pltpu.get_barrier_semaphore()

    def greet(l, t):
        pl.semaphore_signal(barrier, inc=1, device_id=(l, t), device_id_type=MESH)

    def greet_other(l, t):
        @pl.when((l != loop) | (t != chunk))
        def _():
            greet(l, t)

    targets(lambda e, k, h, l, t: greet_other(l, t))
    for i in range(window):
        greet_other(begin + i, slice_home)
    for d in range(1, ring):
        greet(loop_of(expert, plane, lax.rem(spot + d, ring), core), chunk)
    greet(loop_of(expert, 1 - plane, spot, core), chunk)
    greet(loop_of(expert, plane, spot, 1 - core), chunk)

    tokens = loop * block_rows + lax.broadcasted_iota(i32, (block_rows, 1), 0)
    grad = grad_ref[...].astype(f32)
    below = (
        lax.broadcasted_iota(i32, (block_rows, block_rows), 1)
        < lax.broadcasted_iota(i32, (block_rows, block_rows), 0)
    ).astype(f32).astype(bf16)
    slot_lane = lax.broadcasted_iota(i32, (block_rows, SLOTS), 1)
    spread = []
    for e in range(experts):
        same = picks_ref[e : e + 1, :] == tokens
        picked = jnp.sum(jnp.where(same, 1.0, 0.0), axis=1, keepdims=True)
        gate = jnp.sum(jnp.where(same, gates_ref[e : e + 1, :], 0.0), axis=1, keepdims=True)
        wide_picked = jnp.broadcast_to(picked, (block_rows, SLOTS))
        rank = dot_nn(below, wide_picked.astype(bf16)).astype(i32)
        one_hot = jnp.where(
            (rank == slot_lane) & (wide_picked > 0.5), 1.0, 0.0
        ).astype(bf16)
        spread.append(one_hot)
        scaled = (gate * grad).astype(bf16)
        slots = dot_tn(one_hot, scaled).astype(bf16)
        for h in range(halves):
            slot_ref[e, h] = slots[:, h * piece : (h + 1) * piece]

    window_lines = 16 * ((window + 15) // 16)
    block_line = begin + lax.broadcasted_iota(i32, (window_lines, 1), 0)
    earlier = picks_ref[pl.ds(expert, 1), :] < block_line * block_rows
    first_pick = jnp.sum(jnp.where(earlier, 1.0, 0.0), axis=1, keepdims=True).astype(i32)
    block_of = chunk_ref[pl.ds(expert * chunks + chunk, 1), :] // block_rows
    first_row = jnp.sum(
        jnp.where(block_of == block_line, first_pick, 0), axis=0, keepdims=True
    )
    place_of = (
        (block_of - begin) * SLOTS
        + chunk * rows
        + lax.broadcasted_iota(i32, (1, rows), 1)
        - first_row
    )
    select = jnp.where(
        lax.broadcasted_iota(i32, (window * SLOTS, rows), 0) == place_of, 1.0, 0.0
    ).astype(bf16)

    greeted = (
        jnp.where(first + 1 < chunks, jnp.where(start_of(first + 1) <= loop, 1, 0), 0)
        + jnp.where(first + 2 < chunks, jnp.where(start_of(first + 2) <= loop, 1, 0), 0)
        + 1
    )
    own_window = (
        (slice_home == chunk) & (begin <= loop) & (loop < begin + window)
    )
    pl.semaphore_wait(
        barrier,
        greeted * (experts * halves) + window + (ring - 1) + 2 - jnp.where(own_window, 2, 0),
    )

    def a_copy(e, k, h, l, t):
        return pltpu.make_async_remote_copy(
            src_ref=slot_ref.at[e, h],
            dst_ref=arrive_ref.at[loop - start_of(t)],
            send_sem=a_send.at[e, k, h],
            recv_sem=a_recv,
            device_id=(l, t),
            device_id_type=MESH,
        )

    def a_start(e, k, h, l, t):
        @pl.when((l != loop) | (t != chunk))
        def _():
            a_copy(e, k, h, l, t).start()

        @pl.when((l == loop) & (t == chunk))
        def _():
            pltpu.make_async_copy(
                slot_ref.at[e, h], arrive_ref.at[loop - start_of(t)], a_recv
            ).start()

    def a_finish(e, k, h, l, t):
        @pl.when((l != loop) | (t != chunk))
        def _():
            a_copy(e, k, h, l, t).wait_send()

    targets(a_start)
    slope = gelu_slope(hidden_ref[...].astype(f32))
    pltpu.make_async_copy(arrive_ref, arrive_ref, a_recv).wait()
    mine = dot_tn(select, arrive_ref[...].reshape(window * SLOTS, piece)).astype(bf16)
    wide_ref[:, at_slice(core, plane, spot)] = mine

    order = by_distance(ring)

    def bx_copy(d):
        here = wide_ref.at[:, at_slice(core, plane, spot)]
        return pltpu.make_async_remote_copy(
            src_ref=here,
            dst_ref=here,
            send_sem=bx_send.at[d],
            recv_sem=bx_recv.at[d],
            device_id=(loop_of(expert, plane, lax.rem(spot + d, ring), core), chunk),
            device_id_type=MESH,
        )

    def bz_copy(d):
        here = wide_ref.at[:, at_slice(core, plane, lax.rem(spot + ring - d, ring))]
        return pltpu.make_async_remote_copy(
            src_ref=here,
            dst_ref=here,
            send_sem=bz_send.at[d],
            recv_sem=bz_recv.at[d],
            device_id=(loop_of(expert, 1 - plane, spot, core), chunk),
            device_id_type=MESH,
        )

    def bc_copy(p, d):
        other = plane if p == 0 else 1 - plane
        here = wide_ref.at[:, at_slice(core, other, lax.rem(spot + ring - d, ring))]
        return pltpu.make_async_remote_copy(
            src_ref=here,
            dst_ref=here,
            send_sem=bc_send.at[p, d],
            recv_sem=bc_recv.at[p, d],
            device_id=(loop_of(expert, plane, spot, 1 - core), chunk),
            device_id_type=MESH,
        )

    def quarter_of(c, p):
        return pl.ds(pl.multiple_of((c * PLANES + p) * quarter, quarter), quarter)

    def first_product(c, p):
        here = quarter_of(c, p)
        return dot_nt(wide_ref[:, here], out_ref[:, here])

    for d in order:
        bx_copy(d).start()
    bz_copy(0).start()
    bc_copy(0, 0).start()
    for d in order:
        bx_copy(d).wait_recv()
        bz_copy(d).start()
        bc_copy(0, d).start()
    weights[0].wait()
    act = first_product(core, plane)
    for d in [0] + order:
        bz_copy(d).wait_recv()
        bc_copy(1, d).start()
    act += first_product(core, 1 - plane)
    for d in [0] + order:
        bc_copy(0, d).wait_recv()
    act += first_product(1 - core, plane)
    for d in [0] + order:
        bc_copy(1, d).wait_recv()
    act += first_product(1 - core, 1 - plane)
    pre = (act * slope).astype(bf16)

    def second_product(c, p):
        return dot_nt(pre, in_ref[quarter_of(c, p), :])

    def cc_copy(p):
        return pltpu.make_async_remote_copy(
            src_ref=core_send.at[p],
            dst_ref=core_recv.at[p],
            send_sem=cc_send.at[p],
            recv_sem=cc_recv.at[p],
            device_id=(loop_of(expert, plane, spot, 1 - core), chunk),
            device_id_type=MESH,
        )

    def at_spot(s):
        return pl.ds(pl.multiple_of(s * piece, piece), piece)

    def cz_copy(d):
        here = at_spot(lax.rem(spot + d, ring))
        return pltpu.make_async_remote_copy(
            src_ref=plane_send.at[:, here],
            dst_ref=plane_recv.at[:, here],
            send_sem=cz_send.at[d],
            recv_sem=cz_recv.at[d],
            device_id=(loop_of(expert, 1 - plane, spot, core), chunk),
            device_id_type=MESH,
        )

    def cx_copy(d):
        return pltpu.make_async_remote_copy(
            src_ref=ring_send.at[d],
            dst_ref=ring_recv.at[d],
            send_sem=cx_send.at[d],
            recv_sem=cx_recv.at[d],
            device_id=(loop_of(expert, plane, lax.rem(spot + d, ring), core), chunk),
            device_id_type=MESH,
        )

    far_first = list(reversed(order))
    weights[1].wait()
    core_send[1] = second_product(1 - core, 1 - plane).astype(core_send.dtype)
    cc_copy(1).start()
    core_send[0] = second_product(1 - core, plane).astype(core_send.dtype)
    cc_copy(0).start()
    partial = second_product(core, 1 - plane)
    cc_copy(1).wait_recv()
    plane_send[...] = (partial + core_recv[1].astype(f32)).astype(bf16)
    for d in far_first + [0]:
        cz_copy(d).start()
    partial = second_product(core, plane)
    cc_copy(0).wait_recv()
    own_ref[...] = partial + core_recv[0].astype(f32)
    for d in far_first:
        cz_copy(d).wait_recv()
        here = at_spot(lax.rem(spot + d, ring))
        ring_send[d] = (own_ref[:, here] + plane_recv[:, here].astype(f32)).astype(bf16)
        cx_copy(d).start()
    cz_copy(0).wait_recv()
    total = own_ref[:, at_spot(spot)] + plane_recv[:, at_spot(spot)].astype(f32)
    for d in order:
        cx_copy(d).wait_recv()
        total += ring_recv[d].astype(f32)

    high, low = split_exact(total)
    back = dot_nn(select, high) + dot_nn(select, low)
    back_ref[...] = back.reshape(window, SLOTS, piece).astype(back_ref.dtype)

    def d_copy(i):
        home = begin + i
        k = chunk - first_of(home)
        return pltpu.make_async_remote_copy(
            src_ref=back_ref.at[i],
            dst_ref=home_ref.at[expert, k, slice_half],
            send_sem=d_send.at[i],
            recv_sem=d_recv.at[expert, k, slice_half],
            device_id=(home, slice_home),
            device_id_type=MESH,
        )

    def d_start(i):
        home = begin + i

        @pl.when((home != loop) | (slice_home != chunk))
        def _():
            d_copy(i).start()

        @pl.when((home == loop) & (slice_home == chunk))
        def _():
            k = chunk - first_of(home)
            pltpu.make_async_copy(
                back_ref.at[i],
                home_ref.at[expert, k, slice_half],
                d_recv.at[expert, k, slice_half],
            ).start()

    for i in range(window):
        d_start(i)

    targets(a_finish)
    for d in order:
        bx_copy(d).wait_send()
        cx_copy(d).wait_send()
    for d in [0] + order:
        bz_copy(d).wait_send()
        cz_copy(d).wait_send()
        for p in range(PLANES):
            bc_copy(p, d).wait_send()
    for p in range(PLANES):
        cc_copy(p).wait_send()

    def d_wait(e, k, h, l, t):
        pltpu.make_async_copy(
            home_ref.at[e, k, h], home_ref.at[e, k, h], d_recv.at[e, k, h]
        ).wait()

    targets(d_wait)
    moe = jnp.zeros((block_rows, home_cols), f32)
    for e in range(experts):
        parts = []
        for h in range(halves):
            part = home_ref[e, 0, h].astype(f32)
            for k in range(1, CHUNKS):
                part += home_ref[e, k, h].astype(f32)
            parts.append(part)
        high, low = split_exact(jnp.concatenate(parts, axis=1))
        moe += dot_nn(spread[e], high) + dot_nn(spread[e], low)
    result_ref[...] = (grad_ref[...].astype(f32) + moe).astype(result_ref.dtype)
    for i in range(window):
        home = begin + i

        @pl.when((home != loop) | (slice_home != chunk))
        def _():
            d_copy(i).wait_send()


def shards(ring, grad_out, saved_hidden, picked_tokens, gate_values, in_weight, out_weight):
    blocks, chunks = lax.axis_size("loop"), lax.axis_size("tensor")
    experts, capacity = picked_tokens.shape
    rows, width = saved_hidden.shape[0], in_weight.shape[1]
    features = in_weight.shape[0]
    window = window_size(blocks, capacity, chunks)
    group = blocks // experts
    piece = features // group
    halves = group // chunks
    quarter = features // (CORES * PLANES)
    bf16, f32 = jnp.bfloat16, jnp.float32
    vmem, dma = pltpu.VMEM, pltpu.SemaphoreType.DMA
    in_vmem = pl.BlockSpec(memory_space=pltpu.VMEM)
    in_hbm = pl.BlockSpec(memory_space=pl.ANY)
    return pl.pallas_call(
        functools.partial(kernel, (experts, chunks, blocks, ring, window)),
        out_shape=jax.ShapeDtypeStruct(grad_out.shape, bf16),
        in_specs=[in_vmem] * 5 + [in_hbm] * 2,
        out_specs=in_vmem,
        scratch_shapes=[
            vmem((features, width), bf16),
            vmem((width, features), bf16),
            vmem((experts, halves, SLOTS, piece), bf16),
            vmem((window, SLOTS, piece), bf16),
            vmem((rows, features), bf16),
            vmem((PLANES, rows, quarter), bf16),
            vmem((PLANES, rows, quarter), bf16),
            vmem((rows, quarter), bf16),
            vmem((rows, quarter), bf16),
            vmem((rows, quarter), f32),
            vmem((ring, rows, piece), bf16),
            vmem((ring, rows, piece), bf16),
            vmem((window, SLOTS, piece), f32),
            vmem((experts, CHUNKS, halves, SLOTS, piece), f32),
            dma((2,)),
            dma((experts, CHUNKS, halves)),
            dma,
            dma((ring,)),
            dma((ring,)),
            dma((ring,)),
            dma((ring,)),
            dma((PLANES, ring)),
            dma((PLANES, ring)),
            dma((PLANES,)),
            dma((PLANES,)),
            dma((ring,)),
            dma((ring,)),
            dma((ring,)),
            dma((ring,)),
            dma((window,)),
            dma((experts, CHUNKS, halves)),
        ],
        compiler_params=pltpu.CompilerParams(collective_id=0, has_side_effects=True),
    )(
        grad_out,
        saved_hidden,
        picked_tokens,
        gate_values,
        picked_tokens.reshape(experts * chunks, rows),
        in_weight,
        out_weight,
    )


def solution(mesh):
    ring = mesh.shape["loop"] // (2 * PLANES * CORES)
    placed = (
        P("loop", "tensor"),
        P("tensor", "loop"),
        P(),
        P(),
        P(None, "loop"),
        P("loop", None),
    )
    return jax.shard_map(
        functools.partial(shards, ring),
        mesh=mesh,
        in_specs=placed,
        out_specs=P("loop", "tensor"),
        check_vma=False,
    )
```

time: 267 us -> 74.9 us (0.28)
  the two profiles are of different devices: /device:TPU:96 before, /device:TPU:271 now
where the time goes in v1:
time: 74.9 us; the launch traced here: 74.7 us
  Pallas kernels  71.8 us (96%)
  local copies, waits for them, and re-layouts  2.88 us (4%)
    pallas_call x1, Pallas kernels, shards(): pl.pallas_call(functools.partial(kernel, (experts, chunks, blocks, ring,...  71.8 us

profile of v1, /device:TPU:271, one launch (start us, length us, event | category | flops | bytes accessed | tf_op | source)
XLA Modules:
  0.0 74.7 jit_solution(15433606115592779558)
XLA Ops:
  0.0 1.4 %reshape.3.chunk_ref = s32[32,104]{1,0:T(8,128)} reshape(s32[2,1664]{1,0:T(2,128)} %picks_ref.1) | data formatting | bytes 26624 | tf_op jit(solution)/shard_map/reshape | solution.py:527
  1.4 71.8 %shard_map.64 = bf16[128,256]{1,0:T(8,128)(2,1)} custom-call(bf16[128,256]{1,0:T(8,128)(2,1)} %grad_ref.1, bf16[104,512]{1,0:T(8,128)(2,1)} %hidden_ref.1, s32[2,1664]{1,0:T(2,128)} %picks_ref.1, f32[2,1664]{1,0:T(2,128)} %gates_ref.1, s32[32,104]{1,0:T(8,128)} %reshape.3.chunk_ref, bf16[4096,512]{1,0:T(8,128)(2,1)} %in_hbm.1, bf16[512,4096]{1,0:T(8,128)(2,1)} %out_hbm.1), custom_call_target="tpu_custom_call" | custom-call | tf_op jit(solution)/shard_map/pallas_call | solution.py:483
  73.2 1.5 %copy.8 = bf16[128,256]{1,0:T(8,128)(2,1)} copy(bf16[128,256]{1,0:T(8,128)(2,1)} %shard_map.64) | data formatting | bytes 131072

commit v2 on v1

--- a/solution.py
+++ b/solution.py
@@ -10,6 +10,7 @@
 
 MOST = 28
 SLOTS = 32
+LANES = 128
 CORES = 2
 PLANES = 2
 CHUNKS = 3
@@ -58,22 +59,19 @@
     return lax.dot_general(a, b, (((1,), (0,)), ((), ())), preferred_element_type=jnp.float32)
 
 
-def split_exact(values):
-    high = values.astype(jnp.bfloat16)
-    low = (values - high.astype(jnp.float32)).astype(jnp.bfloat16)
-    return high, low
-
-
 def kernel(
     sizes,
+    grad_hbm,
+    hidden_hbm,
+    picks_hbm,
+    gates_hbm,
+    in_hbm,
+    out_hbm,
+    result_ref,
     grad_ref,
     hidden_ref,
     picks_ref,
     gates_ref,
-    chunk_ref,
-    in_hbm,
-    out_hbm,
-    result_ref,
     in_ref,
     out_ref,
     slot_ref,
@@ -88,6 +86,7 @@
     ring_recv,
     back_ref,
     home_ref,
+    input_sem,
     weight_sem,
     a_send,
     a_recv,
@@ -107,10 +106,10 @@
     d_recv,
 ):
     experts, chunks, blocks, ring, window = sizes
-    block_rows, home_cols = grad_ref.shape
-    rows, width = hidden_ref.shape
-    features = in_ref.shape[0]
-    capacity = picks_ref.shape[1]
+    block_rows, home_cols = grad_hbm.shape
+    rows, width = hidden_hbm.shape
+    features = in_hbm.shape[0]
+    capacity = picks_hbm.shape[1]
     group = blocks // experts
     piece = features // group
     halves = group // chunks
@@ -123,10 +122,6 @@
     plane = place // (ring * CORES)
     spot = lax.rem(place // CORES, ring)
     core = lax.rem(place, CORES)
-    slice_id = core * (PLANES * ring) + plane * ring + spot
-    slice_home = slice_id // halves
-    slice_half = lax.rem(slice_id, halves)
-
     def start_of(t):
         return jnp.minimum(rows * t // MOST, blocks - window)
 
@@ -136,11 +131,31 @@
     def loop_of(e, p, s, c):
         return e * group + (p * ring + s) * CORES + c
 
-    def loop_of_slice(e, j):
-        return loop_of(e, lax.rem(j // ring, PLANES), lax.rem(j, ring), j // (PLANES * ring))
+    def middle(t):
+        return start_of(t) + window // 2
+
+    def near_plane(e, t):
+        return jnp.clip(middle(t) // (ring * CORES) - e * PLANES, 0, PLANES - 1)
+
+    def turn(e, t):
+        return middle(t) // CORES + (experts - 1 - e) * (ring // 2)
+
+    def spot_of_home(e, t, home):
+        return lax.rem(turn(e, t) + 3 * (t // PLANES + ring - home // PLANES), ring)
+
+    def plane_of_home(e, t, home):
+        near = near_plane(e, t)
+        return jnp.where(lax.rem(home, PLANES) == lax.rem(t, PLANES), near, 1 - near)
+
+    def home_of(e, t, p, s):
+        side = lax.rem(t, PLANES)
+        lane = lax.rem(t // PLANES + 3 * (turn(e, t) + ring - s), ring)
+        return lane * PLANES + jnp.where(p == near_plane(e, t), side, 1 - side)
 
     first = first_of(loop)
     begin = start_of(chunk)
+    slice_home = home_of(expert, chunk, plane, spot)
+    slice_half = core
 
     def at_slice(c, p, s):
         return pl.ds(pl.multiple_of((c * (PLANES * ring) + p * ring + s) * piece, piece), piece)
@@ -153,15 +168,12 @@
             def _():
                 for e in range(experts):
                     for h in range(halves):
-                        body(e, k, h, loop_of_slice(e, chunk * halves + h), t)
-
-    weights = (
-        pltpu.make_async_copy(out_hbm, out_ref, weight_sem.at[0]),
-        pltpu.make_async_copy(in_hbm, in_ref, weight_sem.at[1]),
-    )
-    for copy in weights:
-        copy.start()
+                        p, s = plane_of_home(e, t, chunk), spot_of_home(e, t, chunk)
+                        body(e, k, h, loop_of(e, p, s, h), t)
+
     home_ref[...] = jnp.zeros_like(home_ref)
+    arrive_ref[...] = jnp.zeros_like(arrive_ref)
+    used = pl.ds(0, MOST)
 
     barrier = pltpu.get_barrier_semaphore()
 
@@ -181,6 +193,22 @@
     greet(loop_of(expert, 1 - plane, spot, core), chunk)
     greet(loop_of(expert, plane, spot, 1 - core), chunk)
 
+    inputs = [
+        pltpu.make_async_copy(here, there, input_sem.at[i])
+        for i, (here, there) in enumerate(
+            (
+                (picks_hbm, picks_ref),
+                (gates_hbm, gates_ref),
+                (grad_hbm, grad_ref),
+                (hidden_hbm, hidden_ref),
+            )
+        )
+    ]
+    for copy in inputs:
+        copy.start()
+
+    for copy in inputs:
+        copy.wait()
     tokens = loop * block_rows + lax.broadcasted_iota(i32, (block_rows, 1), 0)
     grad = grad_ref[...].astype(f32)
     below = (
@@ -208,7 +236,21 @@
     block_line = begin + lax.broadcasted_iota(i32, (window_lines, 1), 0)
     earlier = picks_ref[pl.ds(expert, 1), :] < block_line * block_rows
     first_pick = jnp.sum(jnp.where(earlier, 1.0, 0.0), axis=1, keepdims=True).astype(i32)
-    block_of = chunk_ref[pl.ds(expert * chunks + chunk, 1), :] // block_rows
+    tile = chunk * rows // LANES
+    shift = chunk * rows - tile * LANES
+    last = capacity // LANES - 1
+    lane = lax.broadcasted_iota(i32, (8, LANES), 1)
+
+    def picks_tile(i):
+        here = pl.ds(pl.multiple_of(jnp.minimum(i, last) * LANES, LANES), LANES)
+        row = picks_ref[0:1, here]
+        for e in range(1, experts):
+            row = jnp.where(expert == e, picks_ref[e : e + 1, here], row)
+        wide = jnp.broadcast_to(row, (8, LANES))
+        return pltpu.roll(wide, lax.rem(LANES - shift, LANES), 1)
+
+    own_picks = jnp.where(lane < LANES - shift, picks_tile(tile), picks_tile(tile + 1))
+    block_of = own_picks[0:1, 0:rows] // block_rows
     first_row = jnp.sum(
         jnp.where(block_of == block_line, first_pick, 0), axis=0, keepdims=True
     )
@@ -222,6 +264,7 @@
         lax.broadcasted_iota(i32, (window * SLOTS, rows), 0) == place_of, 1.0, 0.0
     ).astype(bf16)
 
+    slope = gelu_slope(hidden_ref[...].astype(f32))
     greeted = (
         jnp.where(first + 1 < chunks, jnp.where(start_of(first + 1) <= loop, 1, 0), 0)
         + jnp.where(first + 2 < chunks, jnp.where(start_of(first + 2) <= loop, 1, 0), 0)
@@ -237,8 +280,8 @@
 
     def a_copy(e, k, h, l, t):
         return pltpu.make_async_remote_copy(
-            src_ref=slot_ref.at[e, h],
-            dst_ref=arrive_ref.at[loop - start_of(t)],
+            src_ref=slot_ref.at[e, h, used],
+            dst_ref=arrive_ref.at[loop - start_of(t), used],
             send_sem=a_send.at[e, k, h],
             recv_sem=a_recv,
             device_id=(l, t),
@@ -253,7 +296,7 @@
         @pl.when((l == loop) & (t == chunk))
         def _():
             pltpu.make_async_copy(
-                slot_ref.at[e, h], arrive_ref.at[loop - start_of(t)], a_recv
+                slot_ref.at[e, h, used], arrive_ref.at[loop - start_of(t), used], a_recv
             ).start()
 
     def a_finish(e, k, h, l, t):
@@ -262,8 +305,25 @@
             a_copy(e, k, h, l, t).wait_send()
 
     targets(a_start)
-    slope = gelu_slope(hidden_ref[...].astype(f32))
-    pltpu.make_async_copy(arrive_ref, arrive_ref, a_recv).wait()
+
+    for c in range(CORES):
+        for p in range(PLANES):
+            for s in range(ring):
+                t = home_of(expert, chunk, p, s)
+                source = pl.ds(pl.multiple_of((t * CORES + c) * piece, piece), piece)
+                target = pl.ds((c * (PLANES * ring) + p * ring + s) * piece, piece)
+                pltpu.make_async_copy(
+                    out_hbm.at[:, source], out_ref.at[:, target], weight_sem.at[0]
+                ).start()
+                pltpu.make_async_copy(
+                    in_hbm.at[source, :], in_ref.at[target, :], weight_sem.at[1]
+                ).start()
+    weights = (
+        pltpu.make_async_copy(out_ref, out_ref, weight_sem.at[0]),
+        pltpu.make_async_copy(in_ref, in_ref, weight_sem.at[1]),
+    )
+    everything = arrive_ref.at[:, used]
+    pltpu.make_async_copy(everything, everything, a_recv).wait()
     mine = dot_tn(select, arrive_ref[...].reshape(window * SLOTS, piece)).astype(bf16)
     wide_ref[:, at_slice(core, plane, spot)] = mine
 
@@ -394,16 +454,15 @@
         cx_copy(d).wait_recv()
         total += ring_recv[d].astype(f32)
 
-    high, low = split_exact(total)
-    back = dot_nn(select, high) + dot_nn(select, low)
-    back_ref[...] = back.reshape(window, SLOTS, piece).astype(back_ref.dtype)
+    back = dot_nn(select, total.astype(bf16)).astype(bf16)
+    back_ref[...] = back.reshape(window, SLOTS, piece)
 
     def d_copy(i):
         home = begin + i
         k = chunk - first_of(home)
         return pltpu.make_async_remote_copy(
-            src_ref=back_ref.at[i],
-            dst_ref=home_ref.at[expert, k, slice_half],
+            src_ref=back_ref.at[i, used],
+            dst_ref=home_ref.at[expert, k, slice_half, used],
             send_sem=d_send.at[i],
             recv_sem=d_recv.at[expert, k, slice_half],
             device_id=(home, slice_home),
@@ -421,8 +480,8 @@
         def _():
             k = chunk - first_of(home)
             pltpu.make_async_copy(
-                back_ref.at[i],
-                home_ref.at[expert, k, slice_half],
+                back_ref.at[i, used],
+                home_ref.at[expert, k, slice_half, used],
                 d_recv.at[expert, k, slice_half],
             ).start()
 
@@ -443,7 +502,7 @@
 
     def d_wait(e, k, h, l, t):
         pltpu.make_async_copy(
-            home_ref.at[e, k, h], home_ref.at[e, k, h], d_recv.at[e, k, h]
+            home_ref.at[e, k, h, used], home_ref.at[e, k, h, used], d_recv.at[e, k, h]
         ).wait()
 
     targets(d_wait)
@@ -455,8 +514,7 @@
             for k in range(1, CHUNKS):
                 part += home_ref[e, k, h].astype(f32)
             parts.append(part)
-        high, low = split_exact(jnp.concatenate(parts, axis=1))
-        moe += dot_nn(spread[e], high) + dot_nn(spread[e], low)
+        moe += dot_nn(spread[e], jnp.concatenate(parts, axis=1).astype(bf16))
     result_ref[...] = (grad_ref[...].astype(f32) + moe).astype(result_ref.dtype)
     for i in range(window):
         home = begin + i
@@ -483,9 +541,13 @@
     return pl.pallas_call(
         functools.partial(kernel, (experts, chunks, blocks, ring, window)),
         out_shape=jax.ShapeDtypeStruct(grad_out.shape, bf16),
-        in_specs=[in_vmem] * 5 + [in_hbm] * 2,
+        in_specs=[in_hbm] * 6,
         out_specs=in_vmem,
         scratch_shapes=[
+            vmem(grad_out.shape, bf16),
+            vmem(saved_hidden.shape, bf16),
+            vmem(picked_tokens.shape, jnp.int32),
+            vmem(gate_values.shape, f32),
             vmem((features, width), bf16),
             vmem((width, features), bf16),
             vmem((experts, halves, SLOTS, piece), bf16),
@@ -498,8 +560,9 @@
             vmem((rows, quarter), f32),
             vmem((ring, rows, piece), bf16),
             vmem((ring, rows, piece), bf16),
-            vmem((window, SLOTS, piece), f32),
-            vmem((experts, CHUNKS, halves, SLOTS, piece), f32),
+            vmem((window, SLOTS, piece), bf16),
+            vmem((experts, CHUNKS, halves, SLOTS, piece), bf16),
+            dma((4,)),
             dma((2,)),
             dma((experts, CHUNKS, halves)),
             dma,
@@ -524,7 +587,6 @@
         saved_hidden,
         picked_tokens,
         gate_values,
-        picked_tokens.reshape(experts * chunks, rows),
         in_weight,
         out_weight,
     )

time: 74.9 us -> 67.9 us (0.907)
  the two profiles are of different devices: /device:TPU:271 before, /device:TPU:273 now
where the time goes in v2:
time: 67.9 us; the launch traced here: 67.7 us
  Pallas kernels  66.2 us (97%)
  local copies, waits for them, and re-layouts  1.47 us (2%)
    pallas_call x1, Pallas kernels, shards(): pl.pallas_call(functools.partial(kernel, (experts, chunks, blocks, ring,...  66.2 us
    unnamed x1, local copies, waits for them, and re-layouts  1.47 us

profile of v2, /device:TPU:273, one launch (start us, length us, event | category | flops | bytes accessed | tf_op | source)
XLA Modules:
  0.0 67.7 jit_solution(8275952134357635360)
XLA Ops:
  0.0 66.2 %shard_map.64 = bf16[128,256]{1,0:T(8,128)(2,1)} custom-call(bf16[128,256]{1,0:T(8,128)(2,1)} %grad_hbm.1, bf16[104,512]{1,0:T(8,128)(2,1)} %hidden_hbm.1, s32[2,1664]{1,0:T(2,128)} %picks_hbm.1, f32[2,1664]{1,0:T(2,128)} %gates_hbm.1, bf16[4096,512]{1,0:T(8,128)(2,1)} %in_hbm.1, bf16[512,4096]{1,0:T(8,128)(2,1)} %out_hbm.1), custom_call_target="tpu_custom_call" | custom-call | tf_op jit(solution)/shard_map/pallas_call | solution.py:541
  66.2 1.5 %copy.8 = bf16[128,256]{1,0:T(8,128)(2,1)} copy(bf16[128,256]{1,0:T(8,128)(2,1)} %shard_map.64) | data formatting | bytes 131072

commit v3 on v2

--- a/solution.py
+++ b/solution.py
@@ -82,6 +82,8 @@
     plane_send,
     plane_recv,
     own_ref,
+    side_recv,
+    last_send,
     ring_send,
     ring_recv,
     back_ref,
@@ -102,6 +104,8 @@
     cz_recv,
     cx_send,
     cx_recv,
+    cs_send,
+    cs_recv,
     d_send,
     d_recv,
 ):
@@ -340,14 +344,21 @@
             device_id_type=MESH,
         )
 
+    beside = (1, ring - 1) if ring > 2 else ()
+
     def bz_copy(d):
-        here = wide_ref.at[:, at_slice(core, plane, lax.rem(spot + ring - d, ring))]
+        if d in beside:
+            here = wide_ref.at[:, at_slice(core, 1 - plane, spot)]
+            target = loop_of(expert, plane, lax.rem(spot + d, ring), core)
+        else:
+            here = wide_ref.at[:, at_slice(core, plane, lax.rem(spot + ring - d, ring))]
+            target = loop_of(expert, 1 - plane, spot, core)
         return pltpu.make_async_remote_copy(
             src_ref=here,
             dst_ref=here,
             send_sem=bz_send.at[d],
             recv_sem=bz_recv.at[d],
-            device_id=(loop_of(expert, 1 - plane, spot, core), chunk),
+            device_id=(target, chunk),
             device_id_type=MESH,
         )
 
@@ -374,19 +385,28 @@
         bx_copy(d).start()
     bz_copy(0).start()
     bc_copy(0, 0).start()
-    for d in order:
+    for i, d in enumerate(order):
         bx_copy(d).wait_recv()
-        bz_copy(d).start()
+        if i == min(1, len(order) - 1):
+            bz_copy(0).wait_recv()
+            for n in beside:
+                bz_copy(n).start()
+            bc_copy(1, 0).start()
+        if d not in beside:
+            bz_copy(d).start()
         bc_copy(0, d).start()
     weights[0].wait()
     act = first_product(core, plane)
     for d in [0] + order:
+        bc_copy(0, d).wait_recv()
+    act += first_product(1 - core, plane)
+    if not order:
+        bz_copy(0).wait_recv()
+        bc_copy(1, 0).start()
+    for d in order:
         bz_copy(d).wait_recv()
         bc_copy(1, d).start()
     act += first_product(core, 1 - plane)
-    for d in [0] + order:
-        bc_copy(0, d).wait_recv()
-    act += first_product(1 - core, plane)
     for d in [0] + order:
         bc_copy(1, d).wait_recv()
     act += first_product(1 - core, 1 - plane)
@@ -411,7 +431,7 @@
     def cz_copy(d):
         here = at_spot(lax.rem(spot + d, ring))
         return pltpu.make_async_remote_copy(
-            src_ref=plane_send.at[:, here],
+            src_ref=plane_send.at[:, here] if d else last_send,
             dst_ref=plane_recv.at[:, here],
             send_sem=cz_send.at[d],
             recv_sem=cz_recv.at[d],
@@ -429,7 +449,17 @@
             device_id_type=MESH,
         )
 
-    far_first = list(reversed(order))
+    def side_copy(d):
+        return pltpu.make_async_remote_copy(
+            src_ref=plane_send.at[:, at_spot(lax.rem(spot + d, ring))],
+            dst_ref=side_recv.at[beside.index(d)],
+            send_sem=cs_send.at[beside.index(d)],
+            recv_sem=cs_recv.at[beside.index(d)],
+            device_id=(loop_of(expert, plane, lax.rem(spot + d, ring), core), chunk),
+            device_id_type=MESH,
+        )
+
+    far_first = [d for d in reversed(order) if d not in beside]
     weights[1].wait()
     core_send[1] = second_product(1 - core, 1 - plane).astype(core_send.dtype)
     cc_copy(1).start()
@@ -437,12 +467,22 @@
     cc_copy(0).start()
     partial = second_product(core, 1 - plane)
     cc_copy(1).wait_recv()
-    plane_send[...] = (partial + core_recv[1].astype(f32)).astype(bf16)
-    for d in far_first + [0]:
-        cz_copy(d).start()
+    own_ref[...] = partial + core_recv[1].astype(f32)
+    plane_send[...] = own_ref[...].astype(bf16)
+    for d in far_first + list(beside):
+        (side_copy if d in beside else cz_copy)(d).start()
+    here_sum = own_ref[:, at_spot(spot)]
     partial = second_product(core, plane)
     cc_copy(0).wait_recv()
     own_ref[...] = partial + core_recv[0].astype(f32)
+    for d in beside:
+        ring_send[d] = own_ref[:, at_spot(lax.rem(spot + d, ring))].astype(bf16)
+        cx_copy(d).start()
+    for d in beside:
+        side_copy(d).wait_recv()
+        here_sum += side_recv[beside.index(d)].astype(f32)
+    last_send[...] = here_sum.astype(bf16)
+    cz_copy(0).start()
     for d in far_first:
         cz_copy(d).wait_recv()
         here = at_spot(lax.rem(spot + d, ring))
@@ -494,7 +534,7 @@
         cx_copy(d).wait_send()
     for d in [0] + order:
         bz_copy(d).wait_send()
-        cz_copy(d).wait_send()
+        (side_copy if d in beside else cz_copy)(d).wait_send()
         for p in range(PLANES):
             bc_copy(p, d).wait_send()
     for p in range(PLANES):
@@ -540,7 +580,7 @@
     in_hbm = pl.BlockSpec(memory_space=pl.ANY)
     return pl.pallas_call(
         functools.partial(kernel, (experts, chunks, blocks, ring, window)),
-        out_shape=jax.ShapeDtypeStruct(grad_out.shape, bf16),
+        out_shape=pltpu.VMEM(grad_out.shape, bf16),
         in_specs=[in_hbm] * 6,
         out_specs=in_vmem,
         scratch_shapes=[
@@ -558,6 +598,8 @@
             vmem((rows, quarter), bf16),
             vmem((rows, quarter), bf16),
             vmem((rows, quarter), f32),
+            vmem((2, rows, piece), bf16),
+            vmem((rows, piece), bf16),
             vmem((ring, rows, piece), bf16),
             vmem((ring, rows, piece), bf16),
             vmem((window, SLOTS, piece), bf16),
@@ -578,6 +620,8 @@
             dma((ring,)),
             dma((ring,)),
             dma((ring,)),
+            dma((2,)),
+            dma((2,)),
             dma((window,)),
             dma((experts, CHUNKS, halves)),
         ],

time: 67.9 us -> 65.5 us (0.965)
  Pallas kernels: 66.2 us -> 64.6 us
  local copies, waits for them, and re-layouts: 1.47 us -> 0.63 us
    pallas_call x1, Pallas kernels: 66.2 us -> 64.6 us  [shards(): pl.pallas_call(functools.partial(kernel, (experts, chunks, blocks, ring,...]
    unnamed x1, local copies, waits for them, and re-layouts: 1.47 us -> 0.63 us
where the time goes in v3:
time: 65.5 us; the launch traced here: 65.3 us
  Pallas kernels  64.6 us (99%)
    pallas_call x1, Pallas kernels, shards(): pl.pallas_call(functools.partial(kernel, (experts, chunks, blocks, ring,...  64.6 us

profile of v3, /device:TPU:273, one launch (start us, length us, event | category | flops | bytes accessed | tf_op | source)
XLA Modules:
  0.0 65.3 jit_solution(5251208759311005925)
XLA Ops:
  0.0 64.6 %shard_map.64 = bf16[128,256]{1,0:T(8,128)(2,1)S(1)} custom-call(bf16[128,256]{1,0:T(8,128)(2,1)} %grad_hbm.1, bf16[104,512]{1,0:T(8,128)(2,1)} %hidden_hbm.1, s32[2,1664]{1,0:T(2,128)} %picks_hbm.1, f32[2,1664]{1,0:T(2,128)} %gates_hbm.1, bf16[4096,512]{1,0:T(8,128)(2,1)} %in_hbm.1, bf16[512,4096]{1,0:T(8,128)(2,1)} %out_hbm.1), custom_call_target="tpu_custom_call" | custom-call | tf_op jit(solution)/shard_map/pallas_call | solution.py:581
  64.7 0.6 copy.8
